TPU v7x, 256 devices: a whole 4x4x8 slice. The times are simulated.
256 devices in a mesh: gx: 8 (over x_lo, y), gy: 32 (over z, x_hi, core).
Axes of the slice: x: 4 (x_hi: 2, x_lo: 2; x = x_hi * 2 + x_lo), y: 4, z: 8, core: 2. Of those that a mesh axis runs over, the one named last changes fastest.
Arguments:
- plan: int32 [44], replicated, may hold values from 0 to 43, each once
- amplitude: float32 [8, 32, 44, 2, 128], P('gx', 'gy'), may hold values from -12 to 12
- positions: int32 [8, 32, 44, 128], P('gx', 'gy'), may hold values from 0 to 1023
- west_in: bfloat16 [8, 32, 2, 128, 1024], P('gx', 'gy'), may hold values from -6 to 6
- north_in: bfloat16 [8, 32, 2, 128, 1024], P('gx', 'gy'), may hold values from -6 to 6
- corner_now: bfloat16 [8, 32, 2, 128, 128], P('gx', 'gy'), may hold values from -6 to 6
- corner_next: bfloat16 [8, 32, 2, 128, 128], P('gx', 'gy'), may hold values from -6 to 6
- east_map: bfloat16 [8, 32, 2, 1024, 1024], P('gx', 'gy'), may hold values from -0.09375 to 0.09375
- south_map: bfloat16 [8, 32, 2, 1024, 1024], P('gx', 'gy'), may hold values from -0.09375 to 0.09375
Outputs:
- west_out: bfloat16 [8, 32, 2, 128, 1024], P('gx', 'gy')
- north_out: bfloat16 [8, 32, 2, 128, 1024], P('gx', 'gy')
- corner_first: bfloat16 [8, 32, 2, 128, 128], P('gx', 'gy')
- corner_second: bfloat16 [8, 32, 2, 128, 128], P('gx', 'gy')
- interface_residual: float32 [8, 32, 2, 128, 1024], P('gx', 'gy')
Inputs may be any that keep to these rules, and one draw needn't show every extreme that they name: `plan`: a permutation of the 44 batches.
All inputs are finite; a program needn't handle non-finite values.
Results may differ from a plain program's by a relative error of at most 0.015.
Values may be sent and summed in bfloat16 or wider, within the bound.
A program may use at most 64 MiB of HBM per device.

v0:
```python
import jax
import jax.numpy as jnp
from jax import lax
from jax.sharding import PartitionSpec as P

TICKS = 6


def shifted(block, axis, distance):
    devices = range(lax.axis_size(axis))
    route = [(i - distance, i) for i in devices if i - distance in devices]
    return lax.ppermute(block, axis, route)


def padded_2(x, sides, width):
    edges = {}
    for axis, dim in sides:
        size, length = (lax.axis_size(axis), x.shape[dim])
        up = [(i, (i + 1) % size) for i in range(size - 1)]
        last = lax.slice_in_dim(x, length - width, length, axis=dim)
        leading = lax.slice_in_dim(x, 0, width, axis=dim)
        edges[dim] = (
            lax.ppermute(last, axis, up),
            lax.ppermute(leading, axis, [(b, a) for a, b in up]),
        )
    done = []
    for _, dim in sides:
        low, high = edges[dim]
        around = [(width, width) if d in done else (0, 0) for d in range(x.ndim)]
        x = jnp.concatenate([jnp.pad(low, around), x, jnp.pad(high, around)], axis=dim)
        done.append(dim)
    return x


def complex_apply(boundary, maps):
    real = jnp.dot(boundary[0], maps[0], preferred_element_type=jnp.float32) - jnp.dot(
        boundary[1], maps[1], preferred_element_type=jnp.float32
    )
    imag = jnp.dot(boundary[0], maps[1], preferred_element_type=jnp.float32) + jnp.dot(
        boundary[1], maps[0], preferred_element_type=jnp.float32
    )
    return jnp.stack([real, imag], 0).astype(jnp.bfloat16)


def on_device(
    plan, amplitude, positions, west_in, north_in, corner_now, corner_next, east_map, south_map
):
    column = lax.axis_index("gx")
    row = lax.axis_index("gy")
    span = lax.axis_size("gx") + lax.axis_size("gy") - 2
    west = west_in[0, 0]
    north = north_in[0, 0]
    corner_a = corner_now[0, 0]
    corner_b = corner_next[0, 0]
    east_local = east_map[0, 0]
    south_local = south_map[0, 0]
    cell_amps = amplitude[0, 0]
    cell_places = positions[0, 0]
    width = west.shape[-1]
    corner_width = corner_a.shape[-1]
    sources = west.shape[1]
    boundary = west
    for tick in range(TICKS):
        slot = tick - column - row + span
        batch = lax.dynamic_index_in_dim(plan, slot, 0, keepdims=False)
        amps = lax.dynamic_index_in_dim(cell_amps, batch, 0, keepdims=False)
        places = lax.dynamic_index_in_dim(cell_places, batch, 0, keepdims=False)
        points = lax.broadcasted_iota(jnp.int32, (sources, width), 1)
        onehot = (points == places[:, None]).astype(jnp.float32)
        total = (
            west.astype(jnp.float32) + north.astype(jnp.float32) + amps[:, :, None] * onehot[None]
        )
        total = total + jnp.pad(
            corner_a.astype(jnp.float32), ((0, 0), (0, 0), (0, width - corner_width))
        )
        boundary = total.astype(jnp.bfloat16)
        east_out = complex_apply(boundary, east_local)
        south_out = complex_apply(boundary, south_local)
        corner_out = east_out[..., :corner_width]
        west, passing = shifted((east_out, corner_out), "gx", 1)
        north, arrived = shifted((south_out, passing), "gy", 1)
        corner_a = corner_b
        corner_b = arrived
    padded = padded_2(boundary[None, None], (("gx", 0), ("gy", 1)), 1).astype(jnp.float32)
    residual = 4.0 * padded[1, 1] - padded[0, 1] - padded[2, 1] - padded[1, 0] - padded[1, 2]
    return (
        west[None, None],
        north[None, None],
        corner_a[None, None],
        corner_b[None, None],
        residual[None, None],
    )


def solution(mesh):
    return jax.shard_map(
        on_device,
        mesh=mesh,
        in_specs=(
            P(),
            P("gx", "gy", None, None, None),
            P("gx", "gy", None, None),
            P("gx", "gy", None, None, None),
            P("gx", "gy", None, None, None),
            P("gx", "gy", None, None, None),
            P("gx", "gy", None, None, None),
            P("gx", "gy", None, None, None),
            P("gx", "gy", None, None, None),
        ),
        out_specs=(
            P("gx", "gy", None, None, None),
            P("gx", "gy", None, None, None),
            P("gx", "gy", None, None, None),
            P("gx", "gy", None, None, None),
            P("gx", "gy", None, None, None),
        ),
        check_vma=False,
    )
```

profile of v0, /device:TPU:163, one launch (start us, length us, event | category | flops | bytes accessed | tf_op | source)
XLA Modules:
  0.0 237.5 jit_solution(2671403809652107734)
XLA Ops:
  17.3 2.0 fusion.75
  20.8 3.3 %collective-permute-start = (bf16[2,128,1024]{2,1,0:T(8,128)(2,1)S(1)}, bf16[2,128,1024]{2,1,0:T(8,128)(2,1)S(1)}, u32[]{:S(2)}, u32[]{:S(2)}) collective-permute-start(bf16[2,128,1024]{2,1,0:T(8,128)(2,1)S(1)} %pad_maximum_fusion), channel_id=1, source_target_pairs={{0,32},{32,64},{64,96},{96,128},{128,160},{160,192},{192,224},{1,3... | collective-permute-start | bytes 1572872 | tf_op jit(solution)/shard_map/ppermute | solution.py:12
  26.1 4.6 %collective-permute-start.1 = (bf16[2,128,1024]{2,1,0:T(8,128)(2,1)S(1)}, bf16[2,128,1024]{2,1,0:T(8,128)(2,1)S(1)}, u32[]{:S(2)}, u32[]{:S(2)}) collective-permute-start(bf16[2,128,1024]{2,1,0:T(8,128)(2,1)S(1)} %pad_maximum_fusion.6), channel_id=1, source_target_pairs={{0,1},{1,2},{2,3},{3,4},{4,5},{5,6},{6,7},{7,8},{8,9},{9,10},{10,1... | collective-permute-start | bytes 1572872 | tf_op jit(solution)/shard_map/ppermute | solution.py:12
  30.8 6.9 %collective-permute-done = bf16[2,128,1024]{2,1,0:T(8,128)(2,1)S(1)} collective-permute-done((bf16[2,128,1024]{2,1,0:T(8,128)(2,1)S(1)}, bf16[2,128,1024]{2,1,0:T(8,128)(2,1)S(1)}, u32[]{:S(2)}, u32[]{:S(2)}) %collective-permute-start) | collective-permute-done | bytes 524320 | tf_op jit(solution)/shard_map/ppermute | solution.py:12
  40.8 2.2 collective-permute-start.2
  44.1 10.5 %collective-permute-start.3 = (bf16[2,128,1024]{2,1,0:T(8,128)(2,1)S(1)}, bf16[2,128,1024]{2,1,0:T(8,128)(2,1)S(1)}, u32[]{:S(2)}, u32[]{:S(2)}) collective-permute-start(bf16[2,128,1024]{2,1,0:T(8,128)(2,1)S(1)} %pad_maximum_fusion.7), channel_id=1, source_target_pairs={{0,1},{1,2},{2,3},{3,4},{4,5},{5,6},{6,7},{7,8},{8,9},{9,10},{10,1... | collective-permute-start | bytes 1572872 | tf_op jit(solution)/shard_map/ppermute | solution.py:12
  56.5 11.4 %collective-permute-done.4 = bf16[2,128,128]{2,1,0:T(8,128)(2,1)S(1)} collective-permute-done((bf16[2,128,128]{2,1,0:T(8,128)(2,1)S(1)}, bf16[2,128,128]{2,1,0:T(8,128)(2,1)S(1)}, u32[]{:S(2)}, u32[]{:S(2)}) %collective-permute-start.4) | collective-permute-done | bytes 65568 | tf_op jit(solution)/shard_map/ppermute | solution.py:12
  68.0 7.5 %collective-permute-start.5 = (bf16[2,128,128]{2,1,0:T(8,128)(2,1)S(1)}, bf16[2,128,128]{2,1,0:T(8,128)(2,1)S(1)}, u32[]{:S(2)}, u32[]{:S(2)}) collective-permute-start(bf16[2,128,128]{2,1,0:T(8,128)(2,1)S(1)} %collective-permute-done.4), channel_id=1, source_target_pairs={{0,1},{1,2},{2,3},{3,4},{4,5},{5,6},{6,7},{7,8},{8,9},{9,10},{10,1... | collective-permute-start | bytes 196616 | tf_op jit(solution)/shard_map/ppermute | solution.py:12
  82.8 5.8 %collective-permute-start.7 = (bf16[2,128,1024]{2,1,0:T(8,128)(2,1)S(1)}, bf16[2,128,1024]{2,1,0:T(8,128)(2,1)S(1)}, u32[]{:S(2)}, u32[]{:S(2)}) collective-permute-start(bf16[2,128,1024]{2,1,0:T(8,128)(2,1)S(1)} %pad_maximum_fusion.8), channel_id=1, source_target_pairs={{0,1},{1,2},{2,3},{3,4},{4,5},{5,6},{6,7},{7,8},{8,9},{9,10},{10,1... | collective-permute-start | bytes 1572872 | tf_op jit(solution)/shard_map/ppermute | solution.py:12
  90.5 13.7 %collective-permute-done.8 = bf16[2,128,128]{2,1,0:T(8,128)(2,1)S(1)} collective-permute-done((bf16[2,128,128]{2,1,0:T(8,128)(2,1)S(1)}, bf16[2,128,128]{2,1,0:T(8,128)(2,1)S(1)}, u32[]{:S(2)}, u32[]{:S(2)}) %collective-permute-start.8) | collective-permute-done | bytes 65568 | tf_op jit(solution)/shard_map/ppermute | solution.py:12
  104.1 2.5 %collective-permute-start.9 = (bf16[2,128,128]{2,1,0:T(8,128)(2,1)S(1)}, bf16[2,128,128]{2,1,0:T(8,128)(2,1)S(1)}, u32[]{:S(2)}, u32[]{:S(2)}) collective-permute-start(bf16[2,128,128]{2,1,0:T(8,128)(2,1)S(1)} %collective-permute-done.8), channel_id=1, source_target_pairs={{0,1},{1,2},{2,3},{3,4},{4,5},{5,6},{6,7},{7,8},{8,9},{9,10},{10,1... | collective-permute-start | bytes 196616 | tf_op jit(solution)/shard_map/ppermute | solution.py:12
  113.8 5.8 %collective-permute-start.11 = (bf16[2,128,1024]{2,1,0:T(8,128)(2,1)S(1)}, bf16[2,128,1024]{2,1,0:T(8,128)(2,1)S(1)}, u32[]{:S(2)}, u32[]{:S(2)}) collective-permute-start(bf16[2,128,1024]{2,1,0:T(8,128)(2,1)S(1)} %pad_maximum_fusion.9), channel_id=1, source_target_pairs={{0,1},{1,2},{2,3},{3,4},{4,5},{5,6},{6,7},{7,8},{8,9},{9,10},{10,1... | collective-permute-start | bytes 1572872 | tf_op jit(solution)/shard_map/ppermute | solution.py:12
  121.6 14.0 %collective-permute-done.12 = bf16[2,128,128]{2,1,0:T(8,128)(2,1)S(1)} collective-permute-done((bf16[2,128,128]{2,1,0:T(8,128)(2,1)S(1)}, bf16[2,128,128]{2,1,0:T(8,128)(2,1)S(1)}, u32[]{:S(2)}, u32[]{:S(2)}) %collective-permute-start.12) | collective-permute-done | bytes 65568 | tf_op jit(solution)/shard_map/ppermute | solution.py:12
  135.6 2.0 collective-permute-start.13
  144.9 5.8 %collective-permute-start.15 = (bf16[2,128,1024]{2,1,0:T(8,128)(2,1)S(1)}, bf16[2,128,1024]{2,1,0:T(8,128)(2,1)S(1)}, u32[]{:S(2)}, u32[]{:S(2)}) collective-permute-start(bf16[2,128,1024]{2,1,0:T(8,128)(2,1)S(1)} %pad_maximum_fusion.10), channel_id=1, source_target_pairs={{0,1},{1,2},{2,3},{3,4},{4,5},{5,6},{6,7},{7,8},{8,9},{9,10},{10,1... | collective-permute-start | bytes 1572872 | tf_op jit(solution)/shard_map/ppermute | solution.py:12
  154.6 12.8 %collective-permute-done.16 = bf16[2,128,128]{2,1,0:T(8,128)(2,1)S(1)} collective-permute-done((bf16[2,128,128]{2,1,0:T(8,128)(2,1)S(1)}, bf16[2,128,128]{2,1,0:T(8,128)(2,1)S(1)}, u32[]{:S(2)}, u32[]{:S(2)}) %collective-permute-start.16) | collective-permute-done | bytes 65568 | tf_op jit(solution)/shard_map/ppermute | solution.py:12
  172.8 5.8 %collective-permute-start.24 = (bf16[1,1,2,128,1024]{4,3,2,1,0:T(8,128)(2,1)S(1)}, bf16[1,1,2,128,1024]{4,3,2,1,0:T(8,128)(2,1)S(1)}, u32[]{:S(2)}, u32[]{:S(2)}) collective-permute-start(bf16[1,1,2,128,1024]{4,3,2,1,0:T(8,128)(2,1)S(1)} %bitcast.407), channel_id=1, source_target_pairs={{0,1},{1,2},{2,3},{3,4},{4,5},{5,6},{6,7},{7,8},{8,9},{9,10},{10,1... | collective-permute-start | bytes 1572872 | tf_op jit(solution)/shard_map/ppermute | solution.py:23
  180.6 5.5 %collective-permute-start.26 = (bf16[1,1,2,128,1024]{4,3,2,1,0:T(8,128)(2,1)S(1)}, bf16[1,1,2,128,1024]{4,3,2,1,0:T(8,128)(2,1)S(1)}, u32[]{:S(2)}, u32[]{:S(2)}) collective-permute-start(bf16[1,1,2,128,1024]{4,3,2,1,0:T(8,128)(2,1)S(1)} %bitcast.409), channel_id=1, source_target_pairs={{32,0},{64,32},{96,64},{128,96},{160,128},{192,160},{224,192},{33,... | collective-permute-start | bytes 1572872 | tf_op jit(solution)/shard_map/ppermute | solution.py:24
  186.0 3.8 %collective-permute-start.27 = (bf16[1,1,2,128,1024]{4,3,2,1,0:T(8,128)(2,1)S(1)}, bf16[1,1,2,128,1024]{4,3,2,1,0:T(8,128)(2,1)S(1)}, u32[]{:S(2)}, u32[]{:S(2)}) collective-permute-start(bf16[1,1,2,128,1024]{4,3,2,1,0:T(8,128)(2,1)S(1)} %bitcast.410), channel_id=1, source_target_pairs={{1,0},{2,1},{3,2},{4,3},{5,4},{6,5},{7,6},{8,7},{9,8},{10,9},{11,1... | collective-permute-start | bytes 1572872 | tf_op jit(solution)/shard_map/ppermute | solution.py:24
  195.5 7.3 %collective-permute-done.22 = bf16[2,128,128]{2,1,0:T(8,128)(2,1)S(1)} collective-permute-done((bf16[2,128,128]{2,1,0:T(8,128)(2,1)S(1)}, bf16[2,128,128]{2,1,0:T(8,128)(2,1)S(1)}, u32[]{:S(2)}, u32[]{:S(2)}) %collective-permute-start.22) | collective-permute-done | bytes 65568 | tf_op jit(solution)/shard_map/ppermute | solution.py:12
  202.8 7.1 %collective-permute-start.23 = (bf16[2,128,128]{2,1,0:T(8,128)(2,1)S(1)}, bf16[2,128,128]{2,1,0:T(8,128)(2,1)S(1)}, u32[]{:S(2)}, u32[]{:S(2)}) collective-permute-start(bf16[2,128,128]{2,1,0:T(8,128)(2,1)S(1)} %collective-permute-done.22), channel_id=1, source_target_pairs={{0,1},{1,2},{2,3},{3,4},{4,5},{5,6},{6,7},{7,8},{8,9},{9,10},{10,1... | collective-permute-start | bytes 196616 | tf_op jit(solution)/shard_map/ppermute | solution.py:12
  211.2 5.8 %collective-permute-start.19 = (bf16[2,128,1024]{2,1,0:T(8,128)(2,1)S(1)}, bf16[2,128,1024]{2,1,0:T(8,128)(2,1)S(1)}, u32[]{:S(2)}, u32[]{:S(2)}) collective-permute-start(bf16[2,128,1024]{2,1,0:T(8,128)(2,1)S(1)} %pad_maximum_fusion.11), channel_id=1, source_target_pairs={{0,1},{1,2},{2,3},{3,4},{4,5},{5,6},{6,7},{7,8},{8,9},{9,10},{10,1... | collective-permute-start | bytes 1572872 | tf_op jit(solution)/shard_map/ppermute | solution.py:12
  220.1 3.0 %collective-permute-done.19 = bf16[2,128,1024]{2,1,0:T(8,128)(2,1)S(1)} collective-permute-done((bf16[2,128,1024]{2,1,0:T(8,128)(2,1)S(1)}, bf16[2,128,1024]{2,1,0:T(8,128)(2,1)S(1)}, u32[]{:S(2)}, u32[]{:S(2)}) %collective-permute-start.19) | collective-permute-done | bytes 524320 | tf_op jit(solution)/shard_map/ppermute | solution.py:12
  224.6 10.0 %collective-permute-done.18 = bf16[2,128,1024]{2,1,0:T(8,128)(2,1)S(1)} collective-permute-done((bf16[2,128,1024]{2,1,0:T(8,128)(2,1)S(1)}, bf16[2,128,1024]{2,1,0:T(8,128)(2,1)S(1)}, u32[]{:S(2)}, u32[]{:S(2)}) %collective-permute-start.18) | collective-permute-done | bytes 524320 | tf_op jit(solution)/shard_map/ppermute | solution.py:12
  (125 shorter events, 65.3 us)
Async XLA Ops:
  20.8 16.9 %collective-permute-start = (bf16[2,128,1024]{2,1,0:T(8,128)(2,1)S(1)}, bf16[2,128,1024]{2,1,0:T(8,128)(2,1)S(1)}, u32[]{:S(2)}, u32[]{:S(2)}) collective-permute-start(bf16[2,128,1024]{2,1,0:T(8,128)(2,1)S(1)} %pad_maximum_fusion), channel_id=1, source_target_pairs={{0,32},{32,64},{64,96},{96,128},{128,160},{160,192},{192,224},{1,3... | collective-permute-start | bytes 1572872 | tf_op jit(solution)/shard_map/ppermute | solution.py:12
  26.1 11.7 %collective-permute-start.1 = (bf16[2,128,1024]{2,1,0:T(8,128)(2,1)S(1)}, bf16[2,128,1024]{2,1,0:T(8,128)(2,1)S(1)}, u32[]{:S(2)}, u32[]{:S(2)}) collective-permute-start(bf16[2,128,1024]{2,1,0:T(8,128)(2,1)S(1)} %pad_maximum_fusion.6), channel_id=1, source_target_pairs={{0,1},{1,2},{2,3},{3,4},{4,5},{5,6},{6,7},{7,8},{8,9},{9,10},{10,1... | collective-permute-start | bytes 1572872 | tf_op jit(solution)/shard_map/ppermute | solution.py:12
  40.8 35.9 %collective-permute-start.2 = (bf16[2,128,1024]{2,1,0:T(8,128)(2,1)S(1)}, bf16[2,128,1024]{2,1,0:T(8,128)(2,1)S(1)}, u32[]{:S(2)}, u32[]{:S(2)}) collective-permute-start(bf16[2,128,1024]{2,1,0:T(8,128)(2,1)S(1)} %pad_maximum_fusion.1), channel_id=1, source_target_pairs={{0,32},{32,64},{64,96},{96,128},{128,160},{160,192},{192,224},{1,3... | collective-permute-start | bytes 1572872 | tf_op jit(solution)/shard_map/ppermute | solution.py:12
  44.1 32.7 %collective-permute-start.3 = (bf16[2,128,1024]{2,1,0:T(8,128)(2,1)S(1)}, bf16[2,128,1024]{2,1,0:T(8,128)(2,1)S(1)}, u32[]{:S(2)}, u32[]{:S(2)}) collective-permute-start(bf16[2,128,1024]{2,1,0:T(8,128)(2,1)S(1)} %pad_maximum_fusion.7), channel_id=1, source_target_pairs={{0,1},{1,2},{2,3},{3,4},{4,5},{5,6},{6,7},{7,8},{8,9},{9,10},{10,1... | collective-permute-start | bytes 1572872 | tf_op jit(solution)/shard_map/ppermute | solution.py:12
  54.6 13.4 %collective-permute-start.4 = (bf16[2,128,128]{2,1,0:T(8,128)(2,1)S(1)}, bf16[2,128,128]{2,1,0:T(8,128)(2,1)S(1)}, u32[]{:S(2)}, u32[]{:S(2)}) collective-permute-start(bf16[2,128,128]{2,1,0:T(8,128)(2,1)S(1)} %fusion.330), channel_id=1, source_target_pairs={{0,32},{32,64},{64,96},{96,128},{128,160},{160,192},{192,224},{1,3... | collective-permute-start | bytes 196616 | tf_op jit(solution)/shard_map/ppermute | solution.py:12
  68.0 8.8 %collective-permute-start.5 = (bf16[2,128,128]{2,1,0:T(8,128)(2,1)S(1)}, bf16[2,128,128]{2,1,0:T(8,128)(2,1)S(1)}, u32[]{:S(2)}, u32[]{:S(2)}) collective-permute-start(bf16[2,128,128]{2,1,0:T(8,128)(2,1)S(1)} %collective-permute-done.4), channel_id=1, source_target_pairs={{0,1},{1,2},{2,3},{3,4},{4,5},{5,6},{6,7},{7,8},{8,9},{9,10},{10,1... | collective-permute-start | bytes 196616 | tf_op jit(solution)/shard_map/ppermute | solution.py:12
  79.8 28.0 %collective-permute-start.6 = (bf16[2,128,1024]{2,1,0:T(8,128)(2,1)S(1)}, bf16[2,128,1024]{2,1,0:T(8,128)(2,1)S(1)}, u32[]{:S(2)}, u32[]{:S(2)}) collective-permute-start(bf16[2,128,1024]{2,1,0:T(8,128)(2,1)S(1)} %pad_maximum_fusion.2), channel_id=1, source_target_pairs={{0,32},{32,64},{64,96},{96,128},{128,160},{160,192},{192,224},{1,3... | collective-permute-start | bytes 1572872 | tf_op jit(solution)/shard_map/ppermute | solution.py:12
  82.8 25.1 %collective-permute-start.7 = (bf16[2,128,1024]{2,1,0:T(8,128)(2,1)S(1)}, bf16[2,128,1024]{2,1,0:T(8,128)(2,1)S(1)}, u32[]{:S(2)}, u32[]{:S(2)}) collective-permute-start(bf16[2,128,1024]{2,1,0:T(8,128)(2,1)S(1)} %pad_maximum_fusion.8), channel_id=1, source_target_pairs={{0,1},{1,2},{2,3},{3,4},{4,5},{5,6},{6,7},{7,8},{8,9},{9,10},{10,1... | collective-permute-start | bytes 1572872 | tf_op jit(solution)/shard_map/ppermute | solution.py:12
  88.6 15.6 %collective-permute-start.8 = (bf16[2,128,128]{2,1,0:T(8,128)(2,1)S(1)}, bf16[2,128,128]{2,1,0:T(8,128)(2,1)S(1)}, u32[]{:S(2)}, u32[]{:S(2)}) collective-permute-start(bf16[2,128,128]{2,1,0:T(8,128)(2,1)S(1)} %fusion.329), channel_id=1, source_target_pairs={{0,32},{32,64},{64,96},{96,128},{128,160},{160,192},{192,224},{1,3... | collective-permute-start | bytes 196616 | tf_op jit(solution)/shard_map/ppermute | solution.py:12
  110.9 28.0 %collective-permute-start.10 = (bf16[2,128,1024]{2,1,0:T(8,128)(2,1)S(1)}, bf16[2,128,1024]{2,1,0:T(8,128)(2,1)S(1)}, u32[]{:S(2)}, u32[]{:S(2)}) collective-permute-start(bf16[2,128,1024]{2,1,0:T(8,128)(2,1)S(1)} %pad_maximum_fusion.3), channel_id=1, source_target_pairs={{0,32},{32,64},{64,96},{96,128},{128,160},{160,192},{192,224},{1,3... | collective-permute-start | bytes 1572872 | tf_op jit(solution)/shard_map/ppermute | solution.py:12
  113.8 25.1 %collective-permute-start.11 = (bf16[2,128,1024]{2,1,0:T(8,128)(2,1)S(1)}, bf16[2,128,1024]{2,1,0:T(8,128)(2,1)S(1)}, u32[]{:S(2)}, u32[]{:S(2)}) collective-permute-start(bf16[2,128,1024]{2,1,0:T(8,128)(2,1)S(1)} %pad_maximum_fusion.9), channel_id=1, source_target_pairs={{0,1},{1,2},{2,3},{3,4},{4,5},{5,6},{6,7},{7,8},{8,9},{9,10},{10,1... | collective-permute-start | bytes 1572872 | tf_op jit(solution)/shard_map/ppermute | solution.py:12
  119.6 15.9 %collective-permute-start.12 = (bf16[2,128,128]{2,1,0:T(8,128)(2,1)S(1)}, bf16[2,128,128]{2,1,0:T(8,128)(2,1)S(1)}, u32[]{:S(2)}, u32[]{:S(2)}) collective-permute-start(bf16[2,128,128]{2,1,0:T(8,128)(2,1)S(1)} %fusion.328), channel_id=1, source_target_pairs={{0,32},{32,64},{64,96},{96,128},{128,160},{160,192},{192,224},{1,3... | collective-permute-start | bytes 196616 | tf_op jit(solution)/shard_map/ppermute | solution.py:12
  142.0 30.7 %collective-permute-start.14 = (bf16[2,128,1024]{2,1,0:T(8,128)(2,1)S(1)}, bf16[2,128,1024]{2,1,0:T(8,128)(2,1)S(1)}, u32[]{:S(2)}, u32[]{:S(2)}) collective-permute-start(bf16[2,128,1024]{2,1,0:T(8,128)(2,1)S(1)} %pad_maximum_fusion.4), channel_id=1, source_target_pairs={{0,32},{32,64},{64,96},{96,128},{128,160},{160,192},{192,224},{1,3... | collective-permute-start | bytes 1572872 | tf_op jit(solution)/shard_map/ppermute | solution.py:12
  144.9 27.7 %collective-permute-start.15 = (bf16[2,128,1024]{2,1,0:T(8,128)(2,1)S(1)}, bf16[2,128,1024]{2,1,0:T(8,128)(2,1)S(1)}, u32[]{:S(2)}, u32[]{:S(2)}) collective-permute-start(bf16[2,128,1024]{2,1,0:T(8,128)(2,1)S(1)} %pad_maximum_fusion.10), channel_id=1, source_target_pairs={{0,1},{1,2},{2,3},{3,4},{4,5},{5,6},{6,7},{7,8},{8,9},{9,10},{10,1... | collective-permute-start | bytes 1572872 | tf_op jit(solution)/shard_map/ppermute | solution.py:12
  150.7 16.6 %collective-permute-start.16 = (bf16[2,128,128]{2,1,0:T(8,128)(2,1)S(1)}, bf16[2,128,128]{2,1,0:T(8,128)(2,1)S(1)}, u32[]{:S(2)}, u32[]{:S(2)}) collective-permute-start(bf16[2,128,128]{2,1,0:T(8,128)(2,1)S(1)} %fusion.327), channel_id=1, source_target_pairs={{0,32},{32,64},{64,96},{96,128},{128,160},{160,192},{192,224},{1,3... | collective-permute-start | bytes 196616 | tf_op jit(solution)/shard_map/ppermute | solution.py:12
  152.6 16.7 %collective-permute-start.20 = (bf16[2,128,128]{2,1,0:T(8,128)(2,1)S(1)}, bf16[2,128,128]{2,1,0:T(8,128)(2,1)S(1)}, u32[]{:S(2)}, u32[]{:S(2)}) collective-permute-start(bf16[2,128,128]{2,1,0:T(8,128)(2,1)S(1)} %fusion.326), channel_id=1, source_target_pairs={{0,32},{32,64},{64,96},{96,128},{128,160},{160,192},{192,224},{1,3... | collective-permute-start | bytes 196616 | tf_op jit(solution)/shard_map/ppermute | solution.py:12
  172.8 44.1 %collective-permute-start.24 = (bf16[1,1,2,128,1024]{4,3,2,1,0:T(8,128)(2,1)S(1)}, bf16[1,1,2,128,1024]{4,3,2,1,0:T(8,128)(2,1)S(1)}, u32[]{:S(2)}, u32[]{:S(2)}) collective-permute-start(bf16[1,1,2,128,1024]{4,3,2,1,0:T(8,128)(2,1)S(1)} %bitcast.407), channel_id=1, source_target_pairs={{0,1},{1,2},{2,3},{3,4},{4,5},{5,6},{6,7},{7,8},{8,9},{9,10},{10,1... | collective-permute-start | bytes 1572872 | tf_op jit(solution)/shard_map/ppermute | solution.py:23
  178.6 40.3 %collective-permute-start.25 = (bf16[1,1,2,128,1024]{4,3,2,1,0:T(8,128)(2,1)S(1)}, bf16[1,1,2,128,1024]{4,3,2,1,0:T(8,128)(2,1)S(1)}, u32[]{:S(2)}, u32[]{:S(2)}) collective-permute-start(bf16[1,1,2,128,1024]{4,3,2,1,0:T(8,128)(2,1)S(1)} %bitcast.408), channel_id=1, source_target_pairs={{0,32},{32,64},{64,96},{96,128},{128,160},{160,192},{192,224},{1,3... | collective-permute-start | bytes 1572872 | tf_op jit(solution)/shard_map/ppermute | solution.py:23
  180.6 38.4 %collective-permute-start.26 = (bf16[1,1,2,128,1024]{4,3,2,1,0:T(8,128)(2,1)S(1)}, bf16[1,1,2,128,1024]{4,3,2,1,0:T(8,128)(2,1)S(1)}, u32[]{:S(2)}, u32[]{:S(2)}) collective-permute-start(bf16[1,1,2,128,1024]{4,3,2,1,0:T(8,128)(2,1)S(1)} %bitcast.409), channel_id=1, source_target_pairs={{32,0},{64,32},{96,64},{128,96},{160,128},{192,160},{224,192},{33,... | collective-permute-start | bytes 1572872 | tf_op jit(solution)/shard_map/ppermute | solution.py:24
  186.0 32.9 %collective-permute-start.27 = (bf16[1,1,2,128,1024]{4,3,2,1,0:T(8,128)(2,1)S(1)}, bf16[1,1,2,128,1024]{4,3,2,1,0:T(8,128)(2,1)S(1)}, u32[]{:S(2)}, u32[]{:S(2)}) collective-permute-start(bf16[1,1,2,128,1024]{4,3,2,1,0:T(8,128)(2,1)S(1)} %bitcast.410), channel_id=1, source_target_pairs={{1,0},{2,1},{3,2},{4,3},{5,4},{6,5},{7,6},{8,7},{9,8},{10,9},{11,1... | collective-permute-start | bytes 1572872 | tf_op jit(solution)/shard_map/ppermute | solution.py:24
  192.6 10.3 %collective-permute-start.22 = (bf16[2,128,128]{2,1,0:T(8,128)(2,1)S(1)}, bf16[2,128,128]{2,1,0:T(8,128)(2,1)S(1)}, u32[]{:S(2)}, u32[]{:S(2)}) collective-permute-start(bf16[2,128,128]{2,1,0:T(8,128)(2,1)S(1)} %fusion.325), channel_id=1, source_target_pairs={{0,32},{32,64},{64,96},{96,128},{128,160},{160,192},{192,224},{1,3... | collective-permute-start | bytes 196616 | tf_op jit(solution)/shard_map/ppermute | solution.py:12
  202.8 8.4 %collective-permute-start.23 = (bf16[2,128,128]{2,1,0:T(8,128)(2,1)S(1)}, bf16[2,128,128]{2,1,0:T(8,128)(2,1)S(1)}, u32[]{:S(2)}, u32[]{:S(2)}) collective-permute-start(bf16[2,128,128]{2,1,0:T(8,128)(2,1)S(1)} %collective-permute-done.22), channel_id=1, source_target_pairs={{0,1},{1,2},{2,3},{3,4},{4,5},{5,6},{6,7},{7,8},{8,9},{9,10},{10,1... | collective-permute-start | bytes 196616 | tf_op jit(solution)/shard_map/ppermute | solution.py:12
  211.2 11.9 %collective-permute-start.19 = (bf16[2,128,1024]{2,1,0:T(8,128)(2,1)S(1)}, bf16[2,128,1024]{2,1,0:T(8,128)(2,1)S(1)}, u32[]{:S(2)}, u32[]{:S(2)}) collective-permute-start(bf16[2,128,1024]{2,1,0:T(8,128)(2,1)S(1)} %pad_maximum_fusion.11), channel_id=1, source_target_pairs={{0,1},{1,2},{2,3},{3,4},{4,5},{5,6},{6,7},{7,8},{8,9},{9,10},{10,1... | collective-permute-start | bytes 1572872 | tf_op jit(solution)/shard_map/ppermute | solution.py:12
  217.0 17.6 %collective-permute-start.18 = (bf16[2,128,1024]{2,1,0:T(8,128)(2,1)S(1)}, bf16[2,128,1024]{2,1,0:T(8,128)(2,1)S(1)}, u32[]{:S(2)}, u32[]{:S(2)}) collective-permute-start(bf16[2,128,1024]{2,1,0:T(8,128)(2,1)S(1)} %pad_maximum_fusion.5), channel_id=1, source_target_pairs={{0,32},{32,64},{64,96},{96,128},{128,160},{160,192},{192,224},{1,3... | collective-permute-start | bytes 1572872 | tf_op jit(solution)/shard_map/ppermute | solution.py:12
  (7 other events, 38.1 us)
where the time goes:
time: 241 us; the launch traced here: 237 us
  starting transfers between devices  103 us (43%)
  waiting for transfers between devices  85.1 us (35%)
  matrix products  23.5 us (10%)
  between operations  13.2 us (5%)
  other arithmetic  6.56 us (3%)
  local copies, waits for them, and re-layouts  6.35 us (3%)
    ppermute x24, starting transfers between devices, shifted(): return lax.ppermute(block, axis, route)  86 us
    ppermute x24, waiting for transfers between devices, shifted(): return lax.ppermute(block, axis, route)  85 us
    ppermute x2, starting transfers between devices, padded_2(): lax.ppermute(leading, axis, [(b, a) for a, b in up])  9.23 us
    ppermute x2, starting transfers between devices, padded_2(): lax.ppermute(last, axis, up)  7.69 us
    dot_general x12, matrix products, complex_apply(): jnp.dot(boundary[1], maps[1], preferred_element_type=jnp.float32)  6.98 us
    dot_general x12, matrix products, complex_apply(): jnp.dot(boundary[0], maps[0], preferred_element_type=jnp.float32)  5.56 us
    dot_general x12, matrix products, complex_apply(): jnp.dot(boundary[1], maps[0], preferred_element_type=jnp.float32)  5.52 us
    dot_general x12, matrix products, complex_apply(): jnp.dot(boundary[0], maps[1], preferred_element_type=jnp.float32)  5.4 us
  transfers between devices with their start and end apart: 28, of which 13 were waited for; matrix products, arithmetic and copies ran while one was open for 5% of the time, Pallas kernels for 0%

commit v1 on v0

v1 whole, which is shorter than its diff:
```python
import functools

import jax
import jax.numpy as jnp
from jax import lax
from jax.experimental import pallas as pl
from jax.experimental.pallas import tpu as pltpu
from jax.sharding import PartitionSpec as P

MESH = pl.DeviceIdType.MESH
TICKS = 6
GROUPS = 4
LAG = 2
BF16 = jnp.bfloat16
F32 = jnp.float32


def kernel(
    nx,
    ny,
    plan,
    amp_hbm,
    pos_hbm,
    west_hbm,
    north_hbm,
    now_hbm,
    next_hbm,
    east_hbm,
    south_hbm,
    west_out,
    north_out,
    first_out,
    second_out,
    resid_out,
    amp,
    pos,
    maps,
    wbuf,
    nbuf,
    cbuf,
    ebuf,
    fbuf,
    qbuf,
    rbuf,
    relay,
    c1buf,
    c2buf,
    resid,
    rows_s,
    cols_s,
    small_sem,
    map_sem,
    c_sem,
    w_sem,
    n_sem,
    es_sem,
    fs_sem,
    rl_sem,
    rs_sem,
    q_send,
    q_recv,
    k_send,
    k_recv,
    out_sem,
):
    gx = lax.axis_index("gx")
    gy = lax.axis_index("gy")
    G = GROUPS
    R = west_hbm.shape[3] // G
    M = west_hbm.shape[4]
    K = now_hbm.shape[4]
    NC = min(256, M)
    half = nx // 2
    has_w = gx > 0
    has_e = gx < nx - 1
    has_n = gy > 0
    has_s = gy < ny - 1
    east = (gx + 1, gy)
    west = (gx - 1, gy)
    south = (gx, gy + 1)
    north = (gx, gy - 1)
    giver = gx == half - 1
    hub = gx == 0
    taker = gx == half
    hub_dev = (0, gy)
    giver_dev = (half - 1, gy)
    taker_dev = (half, gy)

    barrier = pltpu.get_barrier_semaphore()
    partners = (
        (has_e, east),
        (has_w, west),
        (has_s, south),
        (has_n, north),
        (giver, hub_dev),
        (hub, giver_dev),
        (hub, taker_dev),
        (taker, hub_dev),
    )
    for cond, dev in partners:

        @pl.when(cond)
        def _():
            pl.semaphore_signal(barrier, 1, device_id=dev, device_id_type=MESH)

    amp_copy = pltpu.make_async_copy(amp_hbm.at[0, 0], amp, small_sem.at[0])
    pos_copy = pltpu.make_async_copy(pos_hbm.at[0], pos, small_sem.at[1])
    amp_copy.start()
    pos_copy.start()

    def rows_of(g):
        return pl.ds(g * R, R)

    for g in range(G):
        pltpu.make_async_copy(west_hbm.at[0, 0, :, rows_of(g)], wbuf.at[g], w_sem.at[g]).start()
        pltpu.make_async_copy(north_hbm.at[0, 0, :, rows_of(g)], nbuf.at[g], n_sem.at[g]).start()
    corner_copies = []
    for k, ref in enumerate((now_hbm, next_hbm)):
        for g in range(G):
            corner_copies.append(
                pltpu.make_async_copy(
                    ref.at[0, 0, :, rows_of(g)], cbuf.at[k * G + g], c_sem.at[k * G + g]
                )
            )
    for c in corner_copies:
        c.start()
    map_copies = []
    for k, ref in enumerate((east_hbm, south_hbm)):
        for c in range(2):
            map_copies.append(
                pltpu.make_async_copy(ref.at[0, 0, c], maps.at[k, c], map_sem.at[k * 2 + c])
            )
    for c in map_copies:
        c.start()

    ZW = (TICKS + 1) * G
    wbuf[ZW] = jnp.zeros((2, R, M), BF16)
    nbuf[ZW] = jnp.zeros((2, R, M), BF16)
    ZR = 4 * G
    rbuf[ZR] = jnp.zeros((2, R, M), BF16)

    rows_s[...] = jnp.zeros_like(rows_s)
    amp_copy.wait()
    pos_copy.wait()
    for t in range(TICKS):
        b = plan[t - gx - gy + nx + ny - 2]
        rows_s[8 * t : 8 * t + 2, :] = amp[b]
        rows_s[8 * t + 2 : 8 * t + 3, :] = pos[b].astype(F32)
    flipped = rows_s[...].T
    for t in range(TICKS):
        cols_s[t] = flipped[:, 8 * t : 8 * t + 8]

    def w_index(t, g):
        return jnp.where(hub & (t > 0), ZW, t * G + g)

    def n_index(t, g):
        return jnp.where((gy == 0) & (t > 0), ZW, t * G + g)

    def w_copy(t, g, dev):
        it = t * G + g
        return pltpu.make_async_remote_copy(
            ebuf.at[it],
            wbuf.at[it + G],
            es_sem.at[it],
            w_sem.at[it + G],
            device_id=dev,
            device_id_type=MESH,
        )

    def hub_copy(t, g):
        it = t * G + g
        k = t * (G // 2) + g // 2
        return pltpu.make_async_remote_copy(
            ebuf.at[it],
            relay.at[k],
            es_sem.at[it],
            rl_sem.at[k],
            device_id=hub_dev,
            device_id_type=MESH,
        )

    def onward_copy(t, g):
        it = t * G + g
        k = t * (G // 2) + g // 2
        return pltpu.make_async_remote_copy(
            relay.at[k],
            wbuf.at[it + G],
            rs_sem.at[k],
            w_sem.at[it + G],
            device_id=taker_dev,
            device_id_type=MESH,
        )

    def n_copy(t, g):
        it = t * G + g
        return pltpu.make_async_remote_copy(
            fbuf.at[it],
            nbuf.at[it + G],
            fs_sem.at[it],
            n_sem.at[it + G],
            device_id=south,
            device_id_type=MESH,
        )

    def q_copy(d, g, dev):
        return pltpu.make_async_remote_copy(
            qbuf.at[g],
            rbuf.at[d * G + g],
            q_send.at[d * G + g],
            q_recv.at[d * G + g],
            device_id=dev,
            device_id_type=MESH,
        )

    KQ = TICKS * (G // 2)

    def q_hub_copy(g):
        k = KQ + g // 2
        return pltpu.make_async_remote_copy(
            qbuf.at[g],
            relay.at[k],
            q_send.at[3 * G + g],
            rl_sem.at[k],
            device_id=hub_dev,
            device_id_type=MESH,
        )

    def q_onward_copy(g):
        k = KQ + g // 2
        return pltpu.make_async_remote_copy(
            relay.at[k],
            rbuf.at[3 * G + g],
            rs_sem.at[k],
            q_recv.at[3 * G + g],
            device_id=taker_dev,
            device_id_type=MESH,
        )

    def corner_copy(which, g):
        t = TICKS - 1 + which
        dst = (c1buf, c2buf)[which]
        return pltpu.make_async_remote_copy(
            wbuf.at[w_index(t, g), :, :, pl.ds(0, K)],
            dst.at[g],
            k_send.at[which * G + g],
            k_recv.at[which * G + g],
            device_id=south,
            device_id_type=MESH,
        )

    lanes = lax.broadcasted_iota(jnp.int32, (R, NC), 1).astype(F32)

    def step(it, carry):
        t = it // G
        g = it % G
        odd = g % 2 == 1

        @pl.when(t == 0)
        def _():
            pltpu.make_async_copy(
                west_hbm.at[0, 0, :, pl.ds(pl.multiple_of(g * R, R), R)], wbuf.at[g], w_sem.at[g]
            ).wait()
            pltpu.make_async_copy(
                north_hbm.at[0, 0, :, pl.ds(pl.multiple_of(g * R, R), R)], nbuf.at[g], n_sem.at[g]
            ).wait()

        @pl.when((t > 0) & has_w)
        def _():
            w_copy(t - 1, g, east).wait_recv()

        @pl.when((t > 0) & has_n)
        def _():
            n_copy(t - 1, g).wait_recv()

        @pl.when(it == 0)
        def _():
            for c in corner_copies:
                c.wait()

        wi = w_index(t, g)
        ni = n_index(t, g)
        ci = jnp.minimum(t, 1) * G + g
        cols = cols_s[t, pl.ds(pl.multiple_of(g * R, R), R), :]
        place = cols[:, 2:3]
        for n0 in range(0, M, NC):
            hit = lanes == (place - n0)
            for c in range(2):
                total = wbuf[wi, c, :, n0 : n0 + NC].astype(F32) + nbuf[
                    ni, c, :, n0 : n0 + NC
                ].astype(F32)
                total = total + jnp.where(hit, cols[:, c : c + 1], 0.0)
                if n0 < K:
                    corner = jnp.where(t < 2, cbuf[ci, c].astype(F32), 0.0)
                    qbuf[g, c, :, 0:K] = (total[:, :K] + corner).astype(BF16)
                    if NC > K:
                        qbuf[g, c, :, K:NC] = total[:, K:].astype(BF16)
                else:
                    qbuf[g, c, :, n0 : n0 + NC] = total.astype(BF16)

        def apply(which, dst, fold):
            lhs = qbuf[g].reshape(2 * R, M)
            for n0 in range(0, M, NC):
                a = jnp.dot(lhs, maps[which, 0, :, n0 : n0 + NC], preferred_element_type=F32)
                b = jnp.dot(lhs, maps[which, 1, :, n0 : n0 + NC], preferred_element_type=F32)
                parts = (a[:R] - b[R:], b[:R] + a[R:])
                for c in range(2):
                    part = parts[c]
                    if fold and n0 < K:
                        carried = jnp.where(
                            (t > 0) & (t < TICKS - 1), wbuf[wi, c, :, 0:K].astype(F32), 0.0
                        )
                        dst[it, c, :, 0:K] = (part[:, :K] + carried).astype(BF16)
                        if NC > K:
                            dst[it, c, :, K:NC] = part[:, K:].astype(BF16)
                    else:
                        dst[it, c, :, n0 : n0 + NC] = part.astype(BF16)

        @pl.when(it == 0)
        def _():
            map_copies[0].wait()
            map_copies[1].wait()

        apply(0, ebuf, False)

        @pl.when(it == 0)
        def _():
            count = sum(cond.astype(jnp.int32) for cond, _ in partners)
            pl.semaphore_wait(barrier, count)
            map_copies[2].wait()
            map_copies[3].wait()

        @pl.when(has_e & jnp.logical_not(giver & odd))
        def _():
            w_copy(t, g, east).start()

        @pl.when(giver & odd)
        def _():
            hub_copy(t, g).start()

        @pl.when(t == TICKS - 1)
        def _():
            @pl.when(has_s)
            def _():
                corner_copy(0, g).start()
                q_copy(2, g, south).start()

            @pl.when(has_w)
            def _():
                q_copy(0, g, west).start()

            @pl.when(has_n)
            def _():
                q_copy(1, g, north).start()

        apply(1, fbuf, True)

        @pl.when(has_s)
        def _():
            n_copy(t, g).start()

        back = it - LAG

        @pl.when(hub & (back >= 0) & (back % 2 == 1))
        def _():
            bt = back // G
            bg = back % G
            hub_copy(bt, bg).wait_recv()
            onward_copy(bt, bg).start()

        return carry

    lax.fori_loop(0, TICKS * G, step, 0)

    last = TICKS - 1
    for g in range(G):
        if g % 2 == 1:

            @pl.when(giver)
            def _():
                q_hub_copy(g).start()

        @pl.when(has_e & jnp.logical_not(giver & (g % 2 == 1)))
        def _():
            q_copy(3, g, east).start()

    for back in range(TICKS * G - LAG, TICKS * G):
        if back % 2 == 1:

            @pl.when(hub)
            def _():
                hub_copy(back // G, back % G).wait_recv()
                onward_copy(back // G, back % G).start()

    outs = []

    def put(src, dst, k):
        copy = pltpu.make_async_copy(src, dst, out_sem.at[k])
        copy.start()
        outs.append(copy)

    for g in range(G):

        @pl.when(has_w)
        def _():
            w_copy(last, g, east).wait_recv()

        @pl.when(has_s)
        def _():
            corner_copy(1, g).start()

        put(wbuf.at[w_index(TICKS, g)], west_out.at[0, 0, :, rows_of(g)], g)

    for g in range(G):

        @pl.when(has_n)
        def _():
            n_copy(last, g).wait_recv()

        put(nbuf.at[n_index(TICKS, g)], north_out.at[0, 0, :, rows_of(g)], G + g)

    for which, dst, buf in ((0, first_out, c1buf), (1, second_out, c2buf)):
        for g in range(G):

            @pl.when(has_n)
            def _():
                corner_copy(which, g).wait_recv()

            @pl.when(jnp.logical_not(has_n))
            def _():
                buf[g] = jnp.zeros((2, R, K), BF16)

            put(buf.at[g], dst.at[0, 0, :, rows_of(g)], (2 + which) * G + g)

    for g in range(G):
        if g % 2 == 1:

            @pl.when(hub)
            def _():
                q_hub_copy(g).wait_recv()
                q_onward_copy(g).start()

    for g in range(G):
        sides = ((has_e, 0, west), (has_s, 1, north), (has_n, 2, south), (has_w, 3, east))
        for cond, d, dev in sides:

            @pl.when(cond)
            def _():
                q_copy(d, g, dev).wait_recv()

        idx = [jnp.where(cond, d * G + g, ZR) for cond, d, _ in sides]
        for n0 in range(0, M, NC):
            cut = slice(n0, n0 + NC)
            for c in range(2):
                value = 4.0 * qbuf[g, c, :, cut].astype(F32)
                for i in (3, 0, 2, 1):
                    value = value - rbuf[idx[i], c, :, cut].astype(F32)
                resid[g, c, :, cut] = value
        put(resid.at[g], resid_out.at[0, 0, :, rows_of(g)], 4 * G + g)

    def drain(it, carry):
        t = it // G
        g = it % G
        odd = g % 2 == 1

        @pl.when(has_e & jnp.logical_not(giver & odd))
        def _():
            w_copy(t, g, east).wait_send()

        @pl.when(giver & odd)
        def _():
            hub_copy(t, g).wait_send()

        @pl.when(has_s)
        def _():
            n_copy(t, g).wait_send()

        @pl.when(hub & odd)
        def _():
            onward_copy(t, g).wait_send()

        return carry

    lax.fori_loop(0, TICKS * G, drain, 0)
    for g in range(G):

        @pl.when(has_s)
        def _():
            corner_copy(0, g).wait_send()
            corner_copy(1, g).wait_send()
            q_copy(2, g, south).wait_send()

        @pl.when(has_w)
        def _():
            q_copy(0, g, west).wait_send()

        @pl.when(has_n)
        def _():
            q_copy(1, g, north).wait_send()

        if g % 2 == 1:

            @pl.when(giver)
            def _():
                q_hub_copy(g).wait_send()

            @pl.when(hub)
            def _():
                q_onward_copy(g).wait_send()

        @pl.when(has_e & jnp.logical_not(giver & (g % 2 == 1)))
        def _():
            q_copy(3, g, east).wait_send()

    for copy in outs:
        copy.wait()


def solution(mesh):
    nx, ny = mesh.shape["gx"], mesh.shape["gy"]

    def step(plan, amplitude, positions, west, north, now, nxt, east_map, south_map):
        G = GROUPS
        S, M = west.shape[3], west.shape[4]
        K = now.shape[4]
        R = S // G
        hbm = pl.BlockSpec(memory_space=pl.ANY)
        cell = (2, R, M)
        tick_cells = TICKS * G
        out_shape = (
            jax.ShapeDtypeStruct(west.shape, BF16),
            jax.ShapeDtypeStruct(north.shape, BF16),
            jax.ShapeDtypeStruct(now.shape, BF16),
            jax.ShapeDtypeStruct(nxt.shape, BF16),
            jax.ShapeDtypeStruct(west.shape, F32),
        )
        dma = pltpu.SemaphoreType.DMA
        n_relay = (TICKS + 1) * G // 2
        return pl.pallas_call(
            functools.partial(kernel, nx, ny),
            out_shape=out_shape,
            in_specs=[pl.BlockSpec(memory_space=pltpu.SMEM)] + [hbm] * 8,
            out_specs=(hbm,) * 5,
            scratch_shapes=[
                pltpu.VMEM(amplitude.shape[2:], F32),
                pltpu.VMEM((positions.shape[2], 1, S), jnp.int32),
                pltpu.VMEM((2, 2, M, M), BF16),
                pltpu.VMEM((tick_cells + G + 1,) + cell, BF16),
                pltpu.VMEM((tick_cells + G + 1,) + cell, BF16),
                pltpu.VMEM((2 * G, 2, R, K), BF16),
                pltpu.VMEM((tick_cells,) + cell, BF16),
                pltpu.VMEM((tick_cells,) + cell, BF16),
                pltpu.VMEM((G,) + cell, BF16),
                pltpu.VMEM((4 * G + 1,) + cell, BF16),
                pltpu.VMEM((n_relay,) + cell, BF16),
                pltpu.VMEM((G, 2, R, K), BF16),
                pltpu.VMEM((G, 2, R, K), BF16),
                pltpu.VMEM((G,) + cell, F32),
                pltpu.VMEM((S, S), F32),
                pltpu.VMEM((TICKS, S, 8), F32),
                dma((2,)),
                dma((4,)),
                dma((2 * G,)),
                dma((tick_cells + G,)),
                dma((tick_cells + G,)),
                dma((tick_cells,)),
                dma((tick_cells,)),
                dma((n_relay,)),
                dma((n_relay,)),
                dma((4 * G,)),
                dma((4 * G,)),
                dma((2 * G,)),
                dma((2 * G,)),
                dma((5 * G,)),
            ],
            compiler_params=pltpu.CompilerParams(
                collective_id=0, has_side_effects=True, vmem_limit_bytes=60 * 1024 * 1024
            ),
        )(plan, amplitude, jnp.swapaxes(positions, 1, 2), west, north, now, nxt, east_map, south_map)

    wide = P("gx", "gy", None, None, None)
    return jax.shard_map(
        step,
        mesh=mesh,
        in_specs=(P(), wide, P("gx", "gy", None, None)) + (wide,) * 6,
        out_specs=(wide,) * 5,
        check_vma=False,
    )
```

time: 241 us -> 122 us (0.51); the launches traced: 237 us -> 121 us
  Pallas kernels: 0 us -> 112 us
  starting transfers between devices: 103 us -> 0 us
  waiting for transfers between devices: 85.1 us -> 0 us
  matrix products: 23.5 us -> 0 us
  between operations: 13.2 us -> 0.64 us
  other arithmetic: 6.56 us -> 0 us
  local copies, waits for them, and re-layouts: 6.35 us -> 8.99 us
    pallas_call x0 -> x1, Pallas kernels: none -> 112 us  [step(): pl.pallas_call(functools.partial(kernel, nx, ny), out_shape=out_shape, in...]
    ppermute x28 -> x0, starting transfers between devices: 103 us -> none  [the longest x24 86 us: shifted(): return lax.ppermute(block, axis, route)]
    ppermute x28 -> x0, waiting for transfers between devices: 85.1 us -> none  [the longest x24 85 us: shifted(): return lax.ppermute(block, axis, route)]
    dot_general x48 -> x0, matrix products: 23.5 us -> none  [the longest x12 6.98 us: complex_apply(): jnp.dot(boundary[1], maps[1], preferred_element_type=jnp.float32)]
    unnamed x10 -> x5, local copies, waits for them, and re-layouts: 2.86 us -> 8.99 us
    convert_element_type x13 -> x0, other arithmetic: 4.28 us -> none  [the longest x6 2.53 us: on_device(): boundary = total.astype(jnp.bfloat16)]
  transfers between devices with their start and end apart: 28 -> 0, of which waited for: 13 -> 0; matrix products, arithmetic and copies ran while one was open for 5% -> 0% of each run, Pallas kernels for 0% -> 0%
where the time goes in v1:
time: 122 us; the launch traced here: 121 us
  Pallas kernels  112 us (92%)
  local copies, waits for them, and re-layouts  8.99 us (7%)
    pallas_call x1, Pallas kernels, step(): pl.pallas_call(functools.partial(kernel, nx, ny), out_shape=out_shape, in...  112 us
    unnamed x5, local copies, waits for them, and re-layouts  8.99 us

profile of v1, /device:TPU:163, one launch (start us, length us, event | category | flops | bytes accessed | tf_op | source)
XLA Modules:
  0.0 121.3 jit_solution(6019150985934225733)
XLA Ops:
  0.6 111.7 %shard_map.128 = (bf16[1,1,2,128,1024]{4,3,2,1,0:T(8,128)(2,1)}, bf16[1,1,2,128,1024]{4,3,2,1,0:T(8,128)(2,1)}, bf16[1,1,2,128,128]{4,3,2,1,0:T(8,128)(2,1)}, bf...) custom-call(s32[44]{0:T(128)} %plan.1, f32[1,1,44,2,128]{4,3,2,1,0:T(2,128)} %amp_hbm.1, ...), custom_call_target="tpu_custom_call" | custom-call | tf_op jit(solution)/shard_map/pallas_call | solution.py:538
  112.3 1.9 %copy.19 = bf16[1,1,2,128,1024]{4,3,2,1,0:T(8,128)(2,1)} copy(bf16[1,1,2,128,1024]{4,3,2,1,0:T(8,128)(2,1)} %get-tuple-element.10) | data formatting | bytes 1048576
  114.2 1.9 %copy.20 = bf16[1,1,2,128,1024]{4,3,2,1,0:T(8,128)(2,1)} copy(bf16[1,1,2,128,1024]{4,3,2,1,0:T(8,128)(2,1)} %get-tuple-element.11) | data formatting | bytes 1048576
  116.1 1.5 %copy.21 = bf16[1,1,2,128,128]{4,3,2,1,0:T(8,128)(2,1)} copy(bf16[1,1,2,128,128]{4,3,2,1,0:T(8,128)(2,1)} %get-tuple-element.12) | data formatting | bytes 131072
  117.5 1.5 %copy.22 = bf16[1,1,2,128,128]{4,3,2,1,0:T(8,128)(2,1)} copy(bf16[1,1,2,128,128]{4,3,2,1,0:T(8,128)(2,1)} %get-tuple-element.13) | data formatting | bytes 131072
  119.0 2.3 %copy.23 = f32[1,1,2,128,1024]{4,3,2,1,0:T(8,128)} copy(f32[1,1,2,128,1024]{4,3,2,1,0:T(8,128)} %get-tuple-element.14) | data formatting | bytes 2097152

commit v2 on v1

v2 whole, which is shorter than its diff:
```python
import functools

import jax
import jax.numpy as jnp
from jax import lax
from jax.experimental import pallas as pl
from jax.experimental.pallas import tpu as pltpu
from jax.sharding import PartitionSpec as P

MESH = pl.DeviceIdType.MESH
TICKS = 6
GROUPS = 4
LAG = 2
BF16 = jnp.bfloat16
F32 = jnp.float32


def kernel(
    nx,
    ny,
    plan_hbm,
    amp_hbm,
    pos_hbm,
    west_hbm,
    north_hbm,
    now_hbm,
    next_hbm,
    east_hbm,
    south_hbm,
    west_out,
    north_out,
    first_out,
    second_out,
    resid_out,
    plan,
    amp,
    pos,
    maps,
    wbuf,
    nbuf,
    cbuf,
    ebuf,
    fbuf,
    qbuf,
    rbuf,
    relay,
    rows_s,
    cols_s,
    small_sem,
    map_sem,
    c_sem,
    w_sem,
    n_sem,
    es_sem,
    fs_sem,
    rl_sem,
    rs_sem,
    q_send,
    q_recv,
    k_send,
    k_recv,
):
    gx = lax.axis_index("gx")
    gy = lax.axis_index("gy")
    G = GROUPS
    R = west_hbm.shape[3] // G
    M = west_hbm.shape[4]
    K = now_hbm.shape[4]
    NC = min(256, M)
    half = nx // 2
    has_w = gx > 0
    has_e = gx < nx - 1
    has_n = gy > 0
    has_s = gy < ny - 1
    east = (gx + 1, gy)
    west = (gx - 1, gy)
    south = (gx, gy + 1)
    north = (gx, gy - 1)
    giver = gx == half - 1
    taker = gx == half
    hubs = (gx == 0, gx == 1)
    hub_devs = ((0, gy), (1, gy))
    hub = hubs[0] | hubs[1]
    giver_dev = (half - 1, gy)
    taker_dev = (half, gy)
    core = gy % 2

    def way(it):
        return (it + core) % 3

    def straight(it):
        return has_e & jnp.logical_not(giver & (way(it) > 0))

    def relays(it):
        return (hubs[0] & (way(it) == 1)) | (hubs[1] & (way(it) == 2))

    barrier = pltpu.get_barrier_semaphore()
    partners = (
        (has_e, east),
        (has_w, west),
        (has_s, south),
        (has_n, north),
        (giver, hub_devs[0]),
        (giver, hub_devs[1]),
        (hub, giver_dev),
        (hub, taker_dev),
        (taker, hub_devs[0]),
        (taker, hub_devs[1]),
    )
    for cond, dev in partners:

        @pl.when(cond)
        def _():
            pl.semaphore_signal(barrier, 1, device_id=dev, device_id_type=MESH)

    amp_copy = pltpu.make_async_copy(amp_hbm.at[0, 0], amp, small_sem.at[0])
    pos_copy = pltpu.make_async_copy(pos_hbm.at[0], pos, small_sem.at[1])
    plan_copy = pltpu.make_async_copy(plan_hbm, plan, small_sem.at[2])
    plan_copy.start()
    amp_copy.start()
    pos_copy.start()

    def rows_of(g):
        return pl.ds(g * R, R)

    for g in range(G):
        pltpu.make_async_copy(west_hbm.at[0, 0, :, rows_of(g)], wbuf.at[g], w_sem.at[g]).start()
        pltpu.make_async_copy(north_hbm.at[0, 0, :, rows_of(g)], nbuf.at[g], n_sem.at[g]).start()
    corner_copies = []
    for k, ref in enumerate((now_hbm, next_hbm)):
        for g in range(G):
            corner_copies.append(
                pltpu.make_async_copy(
                    ref.at[0, 0, :, rows_of(g)], cbuf.at[k * G + g], c_sem.at[k * G + g]
                )
            )
    for c in corner_copies:
        c.start()
    map_copies = []
    for k, ref in enumerate((east_hbm, south_hbm)):
        for c in range(2):
            map_copies.append(
                pltpu.make_async_copy(ref.at[0, 0, c], maps.at[k, c], map_sem.at[k * 2 + c])
            )
    for c in map_copies:
        c.start()

    ZW = TICKS * G
    wbuf[ZW] = jnp.zeros((2, R, M), BF16)
    nbuf[ZW] = jnp.zeros((2, R, M), BF16)
    ZR = 4 * G
    rbuf[ZR] = jnp.zeros((2, R, M), BF16)

    @pl.when(gx == 0)
    def _():
        west_out[0, 0] = jnp.zeros((2, G * R, M), BF16)

    @pl.when(gy == 0)
    def _():
        north_out[0, 0] = jnp.zeros((2, G * R, M), BF16)
        first_out[0, 0] = jnp.zeros((2, G * R, K), BF16)
        second_out[0, 0] = jnp.zeros((2, G * R, K), BF16)

    rows_s[...] = jnp.zeros_like(rows_s)
    plan_copy.wait()
    amp_copy.wait()
    pos_copy.wait()
    for t in range(TICKS):
        b = plan[t - gx - gy + nx + ny - 2]
        rows_s[8 * t : 8 * t + 2, :] = amp[b]
        rows_s[8 * t + 2 : 8 * t + 3, :] = pos[b].astype(F32)
    flipped = rows_s[...].T
    for t in range(TICKS):
        cols_s[t] = flipped[:, 8 * t : 8 * t + 8]

    def w_index(t, g):
        return jnp.where((gx == 0) & (t > 0), ZW, t * G + g)

    def n_index(t, g):
        return jnp.where((gy == 0) & (t > 0), ZW, t * G + g)

    def land(ref, g):
        return ref.at[0, 0, :, pl.ds(pl.multiple_of(g * R, R), R)]

    def remote(src, dst, send, recv, dev):
        return pltpu.make_async_remote_copy(
            src, dst, send, recv, device_id=dev, device_id_type=MESH
        )

    def w_copy(it, last):
        dst = land(west_out, it % G) if last else wbuf.at[it + G]
        return remote(ebuf.at[it], dst, es_sem.at[it], w_sem.at[it + G], east)

    def hub_copy(it):
        dev = (jnp.maximum(way(it) - 1, 0), gy)
        return remote(ebuf.at[it], relay.at[it], es_sem.at[it], rl_sem.at[it], dev)

    def onward_copy(it, last):
        dst = land(west_out, it % G) if last else wbuf.at[it + G]
        return remote(relay.at[it], dst, rs_sem.at[it], w_sem.at[it + G], taker_dev)

    def n_copy(it, last):
        dst = land(north_out, it % G) if last else nbuf.at[it + G]
        return remote(fbuf.at[it], dst, fs_sem.at[it], n_sem.at[it + G], south)

    def q_copy(d, g, dev):
        k = d * G + g
        return remote(qbuf.at[g], rbuf.at[k], q_send.at[k], q_recv.at[k], dev)

    KQ = TICKS * G

    def q_hub_copy(g):
        k = KQ + g
        dev = (jnp.maximum(way(k) - 1, 0), gy)
        return remote(qbuf.at[g], relay.at[k], q_send.at[3 * G + g], rl_sem.at[k], dev)

    def q_onward_copy(g):
        k = KQ + g
        return remote(
            relay.at[k], rbuf.at[3 * G + g], rs_sem.at[k], q_recv.at[3 * G + g], taker_dev
        )

    def first_copy(g):
        src = wbuf.at[w_index(TICKS - 1, g), :, :, pl.ds(0, K)]
        return remote(src, land(first_out, g), k_send.at[g], k_recv.at[g], south)

    def second_copy(g):
        src = west_out.at[0, 0, :, pl.ds(g * R, R), pl.ds(0, K)]
        return remote(src, land(second_out, g), k_send.at[G + g], k_recv.at[G + g], south)

    def either(last, make, act):
        @pl.when(last)
        def _():
            getattr(make(True), act)()

        @pl.when(jnp.logical_not(last))
        def _():
            getattr(make(False), act)()

    lanes = lax.broadcasted_iota(jnp.int32, (R, NC), 1).astype(F32)

    def step(it, carry):
        t = it // G
        g = it % G
        last = t == TICKS - 1

        @pl.when(t == 0)
        def _():
            pltpu.make_async_copy(
                west_hbm.at[0, 0, :, pl.ds(pl.multiple_of(g * R, R), R)], wbuf.at[g], w_sem.at[g]
            ).wait()
            pltpu.make_async_copy(
                north_hbm.at[0, 0, :, pl.ds(pl.multiple_of(g * R, R), R)], nbuf.at[g], n_sem.at[g]
            ).wait()

        @pl.when((t > 0) & has_w)
        def _():
            w_copy(it - G, False).wait_recv()

        @pl.when((t > 0) & has_n)
        def _():
            n_copy(it - G, False).wait_recv()

        @pl.when(it == 0)
        def _():
            for c in corner_copies:
                c.wait()

        wi = w_index(t, g)
        ni = n_index(t, g)
        ci = jnp.minimum(t, 1) * G + g
        cols = cols_s[t, pl.ds(pl.multiple_of(g * R, R), R), :]
        place = cols[:, 2:3]
        for n0 in range(0, M, NC):
            hit = lanes == (place - n0)
            for c in range(2):
                total = wbuf[wi, c, :, n0 : n0 + NC].astype(F32) + nbuf[
                    ni, c, :, n0 : n0 + NC
                ].astype(F32)
                total = total + jnp.where(hit, cols[:, c : c + 1], 0.0)
                if n0 < K:
                    corner = jnp.where(t < 2, cbuf[ci, c].astype(F32), 0.0)
                    qbuf[g, c, :, 0:K] = (total[:, :K] + corner).astype(BF16)
                    if NC > K:
                        qbuf[g, c, :, K:NC] = total[:, K:].astype(BF16)
                else:
                    qbuf[g, c, :, n0 : n0 + NC] = total.astype(BF16)

        def apply(which, dst, fold):
            lhs = qbuf[g].reshape(2 * R, M)
            for n0 in range(0, M, NC):
                a = jnp.dot(lhs, maps[which, 0, :, n0 : n0 + NC], preferred_element_type=F32)
                b = jnp.dot(lhs, maps[which, 1, :, n0 : n0 + NC], preferred_element_type=F32)
                parts = (a[:R] - b[R:], b[:R] + a[R:])
                for c in range(2):
                    part = parts[c]
                    if fold and n0 < K:
                        carried = jnp.where(
                            (t > 0) & (t < TICKS - 1), wbuf[wi, c, :, 0:K].astype(F32), 0.0
                        )
                        dst[it, c, :, 0:K] = (part[:, :K] + carried).astype(BF16)
                        if NC > K:
                            dst[it, c, :, K:NC] = part[:, K:].astype(BF16)
                    else:
                        dst[it, c, :, n0 : n0 + NC] = part.astype(BF16)

        @pl.when(it == 0)
        def _():
            map_copies[0].wait()
            map_copies[1].wait()

        apply(0, ebuf, False)

        @pl.when(it == 0)
        def _():
            count = sum(cond.astype(jnp.int32) for cond, _ in partners)
            pl.semaphore_wait(barrier, count)
            map_copies[2].wait()
            map_copies[3].wait()

        @pl.when(straight(it))
        def _():
            either(last, functools.partial(w_copy, it), "start")

        @pl.when(giver & (way(it) > 0))
        def _():
            hub_copy(it).start()

        @pl.when(last)
        def _():
            @pl.when(has_s)
            def _():
                first_copy(g).start()
                q_copy(2, g, south).start()

            @pl.when(has_w)
            def _():
                q_copy(0, g, west).start()

            @pl.when(has_n)
            def _():
                q_copy(1, g, north).start()

        apply(1, fbuf, True)

        @pl.when(has_s)
        def _():
            either(last, functools.partial(n_copy, it), "start")

        back = it - LAG

        @pl.when((back >= 0) & relays(back))
        def _():
            hub_copy(back).wait_recv()
            either(back // G == TICKS - 1, functools.partial(onward_copy, back), "start")

        return carry

    lax.fori_loop(0, TICKS * G, step, 0)

    for g in range(G):

        @pl.when(giver & (way(KQ + g) > 0))
        def _():
            q_hub_copy(g).start()

        @pl.when(straight(KQ + g))
        def _():
            q_copy(3, g, east).start()

    for back in range(KQ - LAG, KQ):

        @pl.when(relays(back))
        def _():
            hub_copy(back).wait_recv()
            onward_copy(back, True).start()

    for g in range(G):

        @pl.when(relays(KQ + g))
        def _():
            q_hub_copy(g).wait_recv()
            q_onward_copy(g).start()

    for g in range(G):

        @pl.when(has_w)
        def _():
            w_copy(KQ - G + g, True).wait_recv()

        @pl.when(has_s)
        def _():
            second_copy(g).start()

    for g in range(G):
        sides = ((has_e, 0, west), (has_s, 1, north), (has_n, 2, south), (has_w, 3, east))
        for cond, d, dev in sides:

            @pl.when(cond)
            def _():
                q_copy(d, g, dev).wait_recv()

        idx = [jnp.where(cond, d * G + g, ZR) for cond, d, _ in sides]
        for n0 in range(0, M, NC):
            cut = slice(n0, n0 + NC)
            for c in range(2):
                value = 4.0 * qbuf[g, c, :, cut].astype(F32)
                for i in (3, 0, 2, 1):
                    value = value - rbuf[idx[i], c, :, cut].astype(F32)
                resid_out[0, 0, c, g * R : (g + 1) * R, cut] = value

    for g in range(G):

        @pl.when(has_n)
        def _():
            n_copy(KQ - G + g, True).wait_recv()
            first_copy(g).wait_recv()
            second_copy(g).wait_recv()

    def drain(it, carry):
        last = it // G == TICKS - 1

        @pl.when(straight(it))
        def _():
            either(last, functools.partial(w_copy, it), "wait_send")

        @pl.when(giver & (way(it) > 0))
        def _():
            hub_copy(it).wait_send()

        @pl.when(has_s)
        def _():
            either(last, functools.partial(n_copy, it), "wait_send")

        @pl.when(relays(it))
        def _():
            either(last, functools.partial(onward_copy, it), "wait_send")

        return carry

    lax.fori_loop(0, TICKS * G, drain, 0)
    for g in range(G):

        @pl.when(has_s)
        def _():
            first_copy(g).wait_send()
            second_copy(g).wait_send()
            q_copy(2, g, south).wait_send()

        @pl.when(has_w)
        def _():
            q_copy(0, g, west).wait_send()

        @pl.when(has_n)
        def _():
            q_copy(1, g, north).wait_send()

        @pl.when(giver & (way(KQ + g) > 0))
        def _():
            q_hub_copy(g).wait_send()

        @pl.when(relays(KQ + g))
        def _():
            q_onward_copy(g).wait_send()

        @pl.when(straight(KQ + g))
        def _():
            q_copy(3, g, east).wait_send()


def write_out(*refs):
    copies = [pltpu.make_async_copy(refs[k], refs[5 + k], refs[10].at[k]) for k in range(5)]
    for copy in copies:
        copy.start()
    for copy in copies:
        copy.wait()


def solution(mesh):
    nx, ny = mesh.shape["gx"], mesh.shape["gy"]

    def step(plan, amplitude, positions, west, north, now, nxt, east_map, south_map):
        G = GROUPS
        S, M = west.shape[3], west.shape[4]
        K = now.shape[4]
        R = S // G
        cell = (2, R, M)
        tick_cells = TICKS * G
        shapes = (
            (west.shape, BF16),
            (north.shape, BF16),
            (now.shape, BF16),
            (nxt.shape, BF16),
            (west.shape, F32),
        )
        out_shape = tuple(pltpu.VMEM(*each) for each in shapes)
        hbm = pl.BlockSpec(memory_space=pltpu.HBM)
        vmem = pl.BlockSpec(memory_space=pltpu.VMEM)
        dma = pltpu.SemaphoreType.DMA
        n_relay = tick_cells + G
        results = pl.pallas_call(
            functools.partial(kernel, nx, ny),
            out_shape=out_shape,
            in_specs=[hbm] * 9,
            out_specs=(vmem,) * 5,
            scratch_shapes=[
                pltpu.SMEM(plan.shape, jnp.int32),
                pltpu.VMEM(amplitude.shape[2:], F32),
                pltpu.VMEM((positions.shape[2], 1, S), jnp.int32),
                pltpu.VMEM((2, 2, M, M), BF16),
                pltpu.VMEM((tick_cells + 1,) + cell, BF16),
                pltpu.VMEM((tick_cells + 1,) + cell, BF16),
                pltpu.VMEM((2 * G, 2, R, K), BF16),
                pltpu.VMEM((tick_cells,) + cell, BF16),
                pltpu.VMEM((tick_cells,) + cell, BF16),
                pltpu.VMEM((G,) + cell, BF16),
                pltpu.VMEM((4 * G + 1,) + cell, BF16),
                pltpu.VMEM((n_relay,) + cell, BF16),
                pltpu.VMEM((S, S), F32),
                pltpu.VMEM((TICKS, S, 8), F32),
                dma((3,)),
                dma((4,)),
                dma((2 * G,)),
                dma((tick_cells + G,)),
                dma((tick_cells + G,)),
                dma((tick_cells,)),
                dma((tick_cells,)),
                dma((n_relay,)),
                dma((n_relay,)),
                dma((4 * G,)),
                dma((4 * G,)),
                dma((2 * G,)),
                dma((2 * G,)),
            ],
            compiler_params=pltpu.CompilerParams(
                collective_id=0, has_side_effects=True, vmem_limit_bytes=48 * 1024 * 1024
            ),
        )(
            *(
                pltpu.with_memory_space_constraint(x, pltpu.HBM)
                for x in (
                    plan,
                    amplitude,
                    jnp.swapaxes(positions, 1, 2),
                    west,
                    north,
                    now,
                    nxt,
                    east_map,
                    south_map,
                )
            ),
        )
        return pl.pallas_call(
            write_out,
            out_shape=tuple(jax.ShapeDtypeStruct(*each) for each in shapes),
            in_specs=[vmem] * 5,
            out_specs=(hbm,) * 5,
            scratch_shapes=[dma((5,))],
        )(*(pltpu.with_memory_space_constraint(x, pltpu.VMEM) for x in results))

    wide = P("gx", "gy", None, None, None)
    return jax.shard_map(
        step,
        mesh=mesh,
        in_specs=(P(), wide, P("gx", "gy", None, None)) + (wide,) * 6,
        out_specs=(wide,) * 5,
        check_vma=False,
    )
```

time: 122 us -> 97.7 us (0.80)
  Pallas kernels: 112 us -> 97 us
  local copies, waits for them, and re-layouts: 8.99 us -> 0 us
    pallas_call x1, Pallas kernels: 112 us -> 95.6 us  [step(): pl.pallas_call(functools.partial(kernel, nx, ny), out_shape=out_shape, in...]
    unnamed x5 -> x0, local copies, waits for them, and re-layouts: 8.99 us -> none
    pallas_call x0 -> x1, Pallas kernels: none -> 1.4 us  [step(): pl.pallas_call(write_out, out_shape=tuple((jax.ShapeDtypeStruct(*each) fo...]
where the time goes in v2:
time: 97.7 us; the launch traced here: 97.6 us
  Pallas kernels  97 us (99%)
    pallas_call x1, Pallas kernels, step(): pl.pallas_call(functools.partial(kernel, nx, ny), out_shape=out_shape, in...  95.6 us

profile of v2, /device:TPU:163, one launch (start us, length us, event | category | flops | bytes accessed | tf_op | source)
XLA Modules:
  0.0 97.6 jit_solution(10051935578454230419)
XLA Ops:
  0.6 95.6 %shard_map.128 = (bf16[1,1,2,128,1024]{4,3,2,1,0:T(8,128)(2,1)S(1)}, bf16[1,1,2,128,1024]{4,3,2,1,0:T(8,128)(2,1)S(1)}, bf16[1,1,2,128,128]{4,3,2,1,0:T(8,128)(2...) custom-call(s32[44]{0:T(128)} %plan_hbm.1, f32[1,1,44,2,128]{4,3,2,1,0:T(2,128)} %amp_hbm.1, ...), custom_call_target="tpu_custom_call" | custom-call | tf_op jit(solution)/shard_map/pallas_call | solution.py:501
  96.2 1.4 %shard_map.129 = (bf16[1,1,2,128,1024]{4,3,2,1,0:T(8,128)(2,1)}, bf16[1,1,2,128,1024]{4,3,2,1,0:T(8,128)(2,1)}, bf16[1,1,2,128,128]{4,3,2,1,0:T(8,128)(2,1)}, bf...) custom-call(bf16[1,1,2,128,1024]{4,3,2,1,0:T(8,128)(2,1)S(1)} %get-tuple-element.10.refs_0_, ...), custom_call_target="tpu_custom_call" | custom-call | tf_op jit(solution)/shard_map/pallas_call | solution.py:554

commit v3 on v2

--- a/solution.py
+++ b/solution.py
@@ -10,7 +10,7 @@
 MESH = pl.DeviceIdType.MESH
 TICKS = 6
 GROUPS = 4
-LAG = 2
+HUB_LAG = 1
 BF16 = jnp.bfloat16
 F32 = jnp.float32
 
@@ -44,6 +44,7 @@
     qbuf,
     rbuf,
     relay,
+    bent,
     rows_s,
     cols_s,
     small_sem,
@@ -55,6 +56,8 @@
     fs_sem,
     rl_sem,
     rs_sem,
+    bl_sem,
+    bs_sem,
     q_send,
     q_recv,
     k_send,
@@ -78,15 +81,19 @@
     north = (gx, gy - 1)
     giver = gx == half - 1
     taker = gx == half
+    ender = gx == nx - 1
     hubs = (gx == 0, gx == 1)
     hub_devs = ((0, gy), (1, gy))
     hub = hubs[0] | hubs[1]
-    giver_dev = (half - 1, gy)
     taker_dev = (half, gy)
     core = gy % 2
+    y = gx % half
 
     def way(it):
         return (it + core) % 3
+
+    bends = has_e & (y < half - 1)
+    stops = ((y == 3) | (y == 1), y == 3)
 
     def straight(it):
         return has_e & jnp.logical_not(giver & (way(it) > 0))
@@ -100,9 +107,12 @@
         (has_w, west),
         (has_s, south),
         (has_n, north),
-        (giver, hub_devs[0]),
-        (giver, hub_devs[1]),
-        (hub, giver_dev),
+        (y == 0, (gx + 3, gy)),
+        (y == 3, (gx - 3, gy)),
+        (y == 1, (gx + 2, gy)),
+        (y == 3, (gx - 2, gy)),
+        (ender, (half - 1, gy)),
+        (giver, (nx - 1, gy)),
         (hub, taker_dev),
         (taker, hub_devs[0]),
         (taker, hub_devs[1]),
@@ -188,20 +198,32 @@
         )
 
     def w_copy(it, last):
-        dst = land(west_out, it % G) if last else wbuf.at[it + G]
-        return remote(ebuf.at[it], dst, es_sem.at[it], w_sem.at[it + G], east)
+        k = it
+        dst = land(west_out, k % G) if last else wbuf.at[k + G]
+        return remote(ebuf.at[k], dst, es_sem.at[k], w_sem.at[k + G], east)
 
     def hub_copy(it):
+        k = it
         dev = (jnp.maximum(way(it) - 1, 0), gy)
-        return remote(ebuf.at[it], relay.at[it], es_sem.at[it], rl_sem.at[it], dev)
+        return remote(ebuf.at[k], relay.at[k], es_sem.at[k], rl_sem.at[k], dev)
 
     def onward_copy(it, last):
-        dst = land(west_out, it % G) if last else wbuf.at[it + G]
-        return remote(relay.at[it], dst, rs_sem.at[it], w_sem.at[it + G], taker_dev)
+        k = it
+        dst = land(west_out, k % G) if last else wbuf.at[k + G]
+        return remote(relay.at[k], dst, rs_sem.at[k], w_sem.at[k + G], taker_dev)
 
     def n_copy(it, last):
-        dst = land(north_out, it % G) if last else nbuf.at[it + G]
-        return remote(fbuf.at[it], dst, fs_sem.at[it], n_sem.at[it + G], south)
+        k = it
+        dst = land(north_out, k % G) if last else nbuf.at[k + G]
+        return remote(fbuf.at[k], dst, fs_sem.at[k], n_sem.at[k + G], south)
+
+    def w_recv(k, last):
+        dst = land(west_out, k % G) if last else wbuf.at[k]
+        return remote(ebuf.at[0], dst, es_sem.at[0], w_sem.at[k], east)
+
+    def n_recv(k, last):
+        dst = land(north_out, k % G) if last else nbuf.at[k]
+        return remote(fbuf.at[0], dst, fs_sem.at[0], n_sem.at[k], south)
 
     def q_copy(d, g, dev):
         k = d * G + g
@@ -219,6 +241,26 @@
         return remote(
             relay.at[k], rbuf.at[3 * G + g], rs_sem.at[k], q_recv.at[3 * G + g], taker_dev
         )
+
+    def q_back_copy(g):
+        k = KQ + g
+        return remote(qbuf.at[g], relay.at[k], q_send.at[g], rl_sem.at[k], (nx - 1, gy))
+
+    def q_return_copy(g):
+        k = KQ + g
+        return remote(relay.at[k], rbuf.at[g], rs_sem.at[k], q_recv.at[g], (half - 1, gy))
+
+    def q_bend_copy():
+        d = jnp.where(y == 1, 1, 0)
+        dev = (jnp.where(y < 2, gx - y + 3, gx - 1), gy)
+        return remote(qbuf.at[0], bent.at[d], q_send.at[3 * G], bl_sem.at[d], dev)
+
+    def q_unbend_copy(kind):
+        dev = (jnp.where(y == 1, gx + 2, gx - 2 + kind), gy)
+        return remote(bent.at[kind], rbuf.at[3 * G], bs_sem.at[kind], q_recv.at[3 * G], dev)
+
+    def q_bend_recv(kind):
+        return remote(qbuf.at[0], bent.at[kind], q_send.at[3 * G], bl_sem.at[kind], east)
 
     def first_copy(g):
         src = wbuf.at[w_index(TICKS - 1, g), :, :, pl.ds(0, K)]
@@ -255,11 +297,11 @@
 
         @pl.when((t > 0) & has_w)
         def _():
-            w_copy(it - G, False).wait_recv()
+            w_recv(it, False).wait_recv()
 
         @pl.when((t > 0) & has_n)
         def _():
-            n_copy(it - G, False).wait_recv()
+            n_recv(it, False).wait_recv()
 
         @pl.when(it == 0)
         def _():
@@ -318,7 +360,7 @@
             map_copies[2].wait()
             map_copies[3].wait()
 
-        @pl.when(straight(it))
+        @pl.when(straight(it) & jnp.logical_not(giver))
         def _():
             either(last, functools.partial(w_copy, it), "start")
 
@@ -333,10 +375,18 @@
                 first_copy(g).start()
                 q_copy(2, g, south).start()
 
-            @pl.when(has_w)
+            @pl.when(has_w & jnp.logical_not(taker & (g % 2 == 1)))
             def _():
                 q_copy(0, g, west).start()
 
+            @pl.when(taker & (g % 2 == 1))
+            def _():
+                q_back_copy(g).start()
+
+            @pl.when(bends & (g == 0))
+            def _():
+                q_bend_copy().start()
+
             @pl.when(has_n)
             def _():
                 q_copy(1, g, north).start()
@@ -347,7 +397,11 @@
         def _():
             either(last, functools.partial(n_copy, it), "start")
 
-        back = it - LAG
+        @pl.when(straight(it) & giver)
+        def _():
+            either(last, functools.partial(w_copy, it), "start")
+
+        back = it - HUB_LAG
 
         @pl.when((back >= 0) & relays(back))
         def _():
@@ -364,11 +418,18 @@
         def _():
             q_hub_copy(g).start()
 
-        @pl.when(straight(KQ + g))
+        @pl.when(straight(KQ + g) & (jnp.logical_not(bends) if g == 0 else True))
         def _():
             q_copy(3, g, east).start()
 
-    for back in range(KQ - LAG, KQ):
+    for kind in range(2):
+
+        @pl.when(stops[kind])
+        def _():
+            q_bend_recv(kind).wait_recv()
+            q_unbend_copy(kind).start()
+
+    for back in range(KQ - HUB_LAG, KQ):
 
         @pl.when(relays(back))
         def _():
@@ -382,11 +443,18 @@
             q_hub_copy(g).wait_recv()
             q_onward_copy(g).start()
 
+        if g % 2 == 1:
+
+            @pl.when(ender)
+            def _():
+                q_back_copy(g).wait_recv()
+                q_return_copy(g).start()
+
     for g in range(G):
 
         @pl.when(has_w)
         def _():
-            w_copy(KQ - G + g, True).wait_recv()
+            w_recv(KQ + g, True).wait_recv()
 
         @pl.when(has_s)
         def _():
@@ -413,7 +481,7 @@
 
         @pl.when(has_n)
         def _():
-            n_copy(KQ - G + g, True).wait_recv()
+            n_recv(KQ + g, True).wait_recv()
             first_copy(g).wait_recv()
             second_copy(g).wait_recv()
 
@@ -451,6 +519,12 @@
         def _():
             q_copy(0, g, west).wait_send()
 
+        if g % 2 == 1:
+
+            @pl.when(ender)
+            def _():
+                q_return_copy(g).wait_send()
+
         @pl.when(has_n)
         def _():
             q_copy(1, g, north).wait_send()
@@ -466,6 +540,12 @@
         @pl.when(straight(KQ + g))
         def _():
             q_copy(3, g, east).wait_send()
+
+    for kind in range(2):
+
+        @pl.when(stops[kind])
+        def _():
+            q_unbend_copy(kind).wait_send()
 
 
 def write_out(*refs):
@@ -516,6 +596,7 @@
                 pltpu.VMEM((G,) + cell, BF16),
                 pltpu.VMEM((4 * G + 1,) + cell, BF16),
                 pltpu.VMEM((n_relay,) + cell, BF16),
+                pltpu.VMEM((2,) + cell, BF16),
                 pltpu.VMEM((S, S), F32),
                 pltpu.VMEM((TICKS, S, 8), F32),
                 dma((3,)),
@@ -527,6 +608,8 @@
                 dma((tick_cells,)),
                 dma((n_relay,)),
                 dma((n_relay,)),
+                dma((2,)),
+                dma((2,)),
                 dma((4 * G,)),
                 dma((4 * G,)),
                 dma((2 * G,)),

time: 97.7 us -> 93 us (0.952); the launches traced: 97.6 us -> 91.7 us
  Pallas kernels: 97 us -> 91.1 us
    pallas_call x1, Pallas kernels: 95.6 us -> 89.7 us  [step(): pl.pallas_call(functools.partial(kernel, nx, ny), out_shape=out_shape, in...]
where the time goes in v3:
time: 93 us; the launch traced here: 91.7 us
  Pallas kernels  91.1 us (98%)
    pallas_call x1, Pallas kernels, step(): pl.pallas_call(functools.partial(kernel, nx, ny), out_shape=out_shape, in...  89.7 us

profile of v3, /device:TPU:163, one launch (start us, length us, event | category | flops | bytes accessed | tf_op | source)
XLA Modules:
  0.0 91.7 jit_solution(10115805804800840115)
XLA Ops:
  0.6 89.7 %shard_map.128 = (bf16[1,1,2,128,1024]{4,3,2,1,0:T(8,128)(2,1)S(1)}, bf16[1,1,2,128,1024]{4,3,2,1,0:T(8,128)(2,1)S(1)}, bf16[1,1,2,128,128]{4,3,2,1,0:T(8,128)(2...) custom-call(s32[44]{0:T(128)} %plan_hbm.1, f32[1,1,44,2,128]{4,3,2,1,0:T(2,128)} %amp_hbm.1, ...), custom_call_target="tpu_custom_call" | custom-call | tf_op jit(solution)/shard_map/pallas_call | solution.py:581
  90.3 1.4 %shard_map.129 = (bf16[1,1,2,128,1024]{4,3,2,1,0:T(8,128)(2,1)}, bf16[1,1,2,128,1024]{4,3,2,1,0:T(8,128)(2,1)}, bf16[1,1,2,128,128]{4,3,2,1,0:T(8,128)(2,1)}, bf...) custom-call(bf16[1,1,2,128,1024]{4,3,2,1,0:T(8,128)(2,1)S(1)} %get-tuple-element.10.refs_0_, ...), custom_call_target="tpu_custom_call" | custom-call | tf_op jit(solution)/shard_map/pallas_call | solution.py:637
